TPU v7x, 256 devices: a whole 4x4x8 slice. The times are simulated.
256 devices in a mesh: req: 8 (over y, core), tp: 32 (over z, x).
Axes of the slice: x: 4, y: 4, z: 8, core: 2. Of those that a mesh axis runs over, the one named last changes fastest.
Arguments:
- queries: bfloat16 [1024, 1536], P(('req', 'tp')), may hold values from -8 to 8
- new_kv: bfloat16 [1024, 1024], P(('req', 'tp')), may hold values from -6 to 6
- residual: bfloat16 [1024, 1536], P(('req', 'tp')), may hold values from -6 to 6
- placement: int32 [16], P('req'), may hold values from 0 to 15, as said below
- lengths: int32 [16], P('req'), may hold values from 2 to 4096
- page_table: int32 [16, 1, 32], P('req', None, 'tp'), may hold values from 0 to 1, as said below
- cache_keys: bfloat16 [512, 128, 512], P(('req', 'tp')), may hold values from -6 to 6
- cache_values: bfloat16 [512, 128, 512], P(('req', 'tp')), may hold values from -6 to 6
- parents: int32 [16, 64], P('req'), may hold values from 0 to 62, as said below
- accept_leaf: int32 [16], P('req'), may hold values from 0 to 63
- out_weight: bfloat16 [1536, 1536], replicated, may hold values from -0.15625 to 0.15625
- norm_gain: float32 [1536], replicated, may hold values from 0.1 to 1.9
- router_weight: bfloat16 [1536, 40], replicated, may hold values from -0.15625 to 0.15625
- expert_ids: int32 [1024, 8], P('req'), may hold values from 0 to 39, all different within a row
- gate_up: bfloat16 [160, 1536, 256], P('tp'), may hold values from -0.15625 to 0.15625
- down_weight: bfloat16 [160, 128, 1536], P('tp'), may hold values from -0.25 to 0.25
Outputs:
- attn_out: bfloat16 [1024, 1536], P(('req', 'tp'))
- layer_out: bfloat16 [1024, 1536], P(('req', 'tp'))
- accepted_kv: bfloat16 [1024, 1024], P(('req', 'tp'))
Inputs may be any that keep to these rules, and one draw needn't show every extreme that they name: `placement`: slot s of each group of 2 slots holds a request whose index is s modulo 2; every request is held once. `page_table`: within each group of 2 slots and each last index, the 2 entries are distinct. parents[s, n] < n for n > 0; parents[s, 0] = 0.
All inputs are finite; a program needn't handle non-finite values.
Results may differ from a plain program's by a relative error of at most 0.01.
Values may be sent and summed in bfloat16 or wider, within the bound.
A program may use at most 128 MiB of HBM per device.

v0:
```python
import math
import jax
import jax.numpy as jnp
from jax import lax
from jax.sharding import PartitionSpec as P

HEADS = 24
KV_HEADS = 8
HEAD = 64
FF_E = 512
UNIT = 128
DRAFT = 64
neg_big = -1e30
norm_eps = 1e-06


def joined_2(part, axis, combine):
    gathered = jax.tree.map(lambda a: lax.all_gather(a, axis), part)

    def take(source):
        return jax.tree.map(lambda a: lax.dynamic_index_in_dim(a, source, 0, False), gathered)

    return lax.fori_loop(
        1, lax.axis_size(axis), lambda source, state: combine(state, take(source)), take(0)
    )


def ancestry(parents):
    node_count = parents.shape[-1]
    node_ids = jnp.arange(node_count, dtype=jnp.int32)
    linked = (parents[:, :, None] == node_ids[None, None, :]) & (node_ids[None, :, None] > 0)
    reached = jnp.maximum(linked.astype(jnp.float32), jnp.eye(node_count, dtype=jnp.float32)[None])
    for _ in range(node_count.bit_length()):
        reached = jnp.minimum(
            jnp.einsum("rnm,rmk->rnk", reached, reached, precision=lax.Precision.HIGHEST), 1.0
        )
    return reached


def combine_stats(left_stats, right_stats):
    left_max, left_sum, left_out = left_stats
    right_max, right_sum, right_out = right_stats
    top_score = jnp.maximum(left_max, right_max)
    left_scale = jnp.exp(left_max - top_score)
    right_scale = jnp.exp(right_max - top_score)
    row_count, head_count = left_max.shape
    out_sum = (
        left_out.reshape(row_count, head_count, -1) * left_scale[..., None]
        + right_out.reshape(row_count, head_count, -1) * right_scale[..., None]
    )
    return (
        top_score,
        left_sum * left_scale + right_sum * right_scale,
        out_sum.reshape(row_count, -1),
    )


def finish_rows(stat_sum, stat_out):
    row_count, head_count = stat_sum.shape
    return (
        (stat_out.reshape(row_count, head_count, -1) / stat_sum[..., None])
        .reshape(row_count, -1)
        .astype(jnp.bfloat16)
    )


def project_rows(attn_rows, res_rows, out_weight):
    return res_rows.astype(jnp.float32) + jnp.dot(
        attn_rows, out_weight, preferred_element_type=jnp.float32
    )


def rms_normed(hidden, norm_gain):
    scale_rows = lax.rsqrt(jnp.mean(hidden * hidden, axis=-1, keepdims=True) + norm_eps)
    return (hidden * scale_rows * norm_gain).astype(jnp.bfloat16)


def unit_shares(normed_all, router_weight, expert_ids, tp_rank, units_dev):
    logits = jnp.dot(normed_all, router_weight, preferred_element_type=jnp.float32)
    expert_range = jnp.arange(router_weight.shape[1], dtype=jnp.int32)
    onehot = (expert_ids[:, :, None] == expert_range[None, None, :]).astype(jnp.float32)
    chosen = jnp.sum(logits[:, None, :] * onehot, axis=-1)
    expo_chosen = jnp.exp(chosen)
    expert_probs = expo_chosen / jnp.sum(expo_chosen, axis=-1, keepdims=True)
    routing = jnp.sum(expert_probs[:, :, None] * onehot, axis=1)
    unit_ids = tp_rank * units_dev + jnp.arange(units_dev, dtype=jnp.int32)
    expert_of_unit = unit_ids // (FF_E // UNIT)
    pick = (expert_range[:, None] == expert_of_unit[None, :]).astype(jnp.float32)
    return jnp.dot(routing, pick, precision=lax.Precision.HIGHEST)


def per_device(
    queries,
    new_kv,
    residual,
    placement,
    lengths,
    page_table,
    cache_keys,
    cache_values,
    parents,
    accept_leaf,
    out_weight,
    norm_gain,
    router_weight,
    expert_ids,
    gate_up,
    down_weight,
):
    tok_dev = queries.shape[0]
    tp_count = lax.axis_size("tp")
    tp_rank = lax.axis_index("tp")
    group_rows = tok_dev * tp_count
    slot_count = placement.shape[0]
    kv_width = cache_keys.shape[2]
    page_len = cache_keys.shape[1]
    group_size = HEADS // KV_HEADS
    score_scale = 1.0 / math.sqrt(HEAD)
    row_start = tp_rank * tok_dev
    pulled_q, pulled_kv, pulled_res = (
        lax.all_gather(queries, "req", axis=0, tiled=True),
        lax.all_gather(new_kv, "req", axis=0, tiled=True),
        lax.all_gather(residual, "req", axis=0, tiled=True),
    )
    row_offsets = jnp.arange(tok_dev, dtype=jnp.int32)
    row_pos = row_start + row_offsets
    row_slot = row_pos // DRAFT
    slot_match = row_slot[:, None] == jnp.arange(slot_count, dtype=jnp.int32)[None, :]
    source_group = jnp.sum(jnp.where(slot_match, placement[None, :] // slot_count, 0), axis=1)
    source_rows = source_group * tok_dev + row_offsets
    own_q = jnp.take(pulled_q, source_rows, axis=0)
    own_kv = jnp.take(pulled_kv, source_rows, axis=0)
    own_res = jnp.take(pulled_res, source_rows, axis=0)
    all_q, all_kv = (
        lax.all_gather(own_q, "tp", axis=0, tiled=True),
        lax.all_gather(own_kv, "tp", axis=0, tiled=True),
    )
    local_pages = page_table.shape[1]
    page_ids = page_table[:, :, 0].reshape(-1)
    keys_local = jnp.take(cache_keys, page_ids, axis=0).reshape(
        slot_count, local_pages, page_len, KV_HEADS, HEAD
    )
    values_local = jnp.take(cache_values, page_ids, axis=0).reshape(
        slot_count, local_pages, page_len, KV_HEADS, HEAD
    )
    query_blocks = all_q.reshape(slot_count, DRAFT, KV_HEADS, group_size, HEAD)
    scores = (
        jnp.einsum(
            "sqgrd,sltgd->sqgrlt", query_blocks, keys_local, preferred_element_type=jnp.float32
        )
        * score_scale
    )
    positions = (
        jnp.arange(local_pages, dtype=jnp.int32)[:, None] * tp_count + tp_rank
    ) * page_len + jnp.arange(page_len, dtype=jnp.int32)[None, :]
    is_valid = (positions[None] < lengths[:, None, None])[:, None, None, None]
    scores = jnp.where(is_valid, scores, neg_big)
    block_max = jnp.max(scores, axis=-1)
    weights = jnp.where(is_valid, jnp.exp(scores - block_max[..., None]), 0.0).astype(jnp.bfloat16)
    block_sum = jnp.sum(weights.astype(jnp.float32), axis=-1)
    block_out = jnp.einsum(
        "sqgrlt,sltgd->sqgrld", weights, values_local, preferred_element_type=jnp.float32
    )
    page_top = jnp.max(block_max, axis=-1)
    page_scale = jnp.exp(block_max - page_top[..., None])
    stat_max = page_top.reshape(group_rows, HEADS)
    stat_sum = jnp.sum(block_sum * page_scale, axis=-1).reshape(group_rows, HEADS)
    stat_out = jnp.sum(block_out * page_scale[..., None], axis=-2).reshape(group_rows, HEADS * HEAD)
    reached = ancestry(parents)
    reach_rows = jnp.take(reached.reshape(slot_count * DRAFT, DRAFT), row_pos, axis=0)
    key_slot = jnp.arange(group_rows, dtype=jnp.int32) // DRAFT
    same_slot = key_slot[None, :] == row_slot[:, None]
    allowed = same_slot & (jnp.tile(reach_rows, (1, slot_count)) > 0.5)
    tree_keys = all_kv[:, :kv_width].reshape(group_rows, KV_HEADS, HEAD)
    tree_values = all_kv[:, kv_width:].reshape(group_rows, KV_HEADS, HEAD)
    own_blocks = own_q.reshape(tok_dev, KV_HEADS, group_size, HEAD)
    tree_scores = (
        jnp.einsum("igrd,kgd->igrk", own_blocks, tree_keys, preferred_element_type=jnp.float32)
        * score_scale
    )
    tree_mask = allowed[:, None, None, :]
    tree_scores = jnp.where(tree_mask, tree_scores, neg_big)
    tree_max = jnp.max(tree_scores, axis=-1)
    tree_weights = jnp.where(tree_mask, jnp.exp(tree_scores - tree_max[..., None]), 0.0).astype(
        jnp.bfloat16
    )
    tree_sum = jnp.sum(tree_weights.astype(jnp.float32), axis=-1)
    tree_out = jnp.einsum(
        "igrk,kgd->igrd", tree_weights, tree_values, preferred_element_type=jnp.float32
    )
    own_stats = (
        lax.dynamic_slice_in_dim(stat_max, row_start, tok_dev, 0),
        lax.dynamic_slice_in_dim(stat_sum, row_start, tok_dev, 0),
        lax.dynamic_slice_in_dim(stat_out, row_start, tok_dev, 0),
    )
    tree_stats = (
        tree_max.reshape(tok_dev, HEADS),
        tree_sum.reshape(tok_dev, HEADS),
        tree_out.reshape(tok_dev, HEADS * HEAD),
    )
    joined = combine_stats(own_stats, tree_stats)
    stat_max = lax.dynamic_update_slice_in_dim(stat_max, joined[0], row_start, 0)
    stat_sum = lax.dynamic_update_slice_in_dim(stat_sum, joined[1], row_start, 0)
    stat_out = lax.dynamic_update_slice_in_dim(stat_out, joined[2], row_start, 0)
    normed_all = None
    merged = joined_2((stat_max, stat_sum, stat_out), "tp", combine_stats)
    attn_own = finish_rows(
        lax.dynamic_slice_in_dim(merged[1], row_start, tok_dev, 0),
        lax.dynamic_slice_in_dim(merged[2], row_start, tok_dev, 0),
    )
    hidden_own = project_rows(attn_own, own_res, out_weight)
    normed_own = rms_normed(hidden_own, norm_gain)
    units_dev = gate_up.shape[0]
    unit_width = gate_up.shape[2] // 2
    normed_all = lax.all_gather(normed_own, "tp", axis=0, tiled=True)
    shares = unit_shares(normed_all, router_weight, expert_ids, tp_rank, units_dev)
    gate_both = jnp.einsum("td,udh->tuh", normed_all, gate_up, preferred_element_type=jnp.float32)
    activated = (
        jax.nn.silu(gate_both[..., :unit_width]) * gate_both[..., unit_width:] * shares[:, :, None]
    ).astype(jnp.bfloat16)
    moe_own = lax.psum_scatter(
        jnp.einsum("tuh,uhd->td", activated, down_weight, preferred_element_type=jnp.float32),
        "tp",
        scatter_dimension=0,
        tiled=True,
    )
    layer_out = (hidden_own + moe_own).astype(jnp.bfloat16)
    node_ids = jnp.arange(DRAFT, dtype=jnp.int32)
    leaf_pick = (accept_leaf[:, None] == node_ids[None, :]).astype(jnp.float32)
    path_weight = jnp.einsum("sn,snk->sk", leaf_pick, reached, precision=lax.Precision.HIGHEST)
    path_flags = (path_weight > 0.5).astype(jnp.int32)
    path_rank = jnp.cumsum(path_flags, axis=1) - 1
    chosen_node = (path_flags[:, None, :] > 0) & (path_rank[:, None, :] == node_ids[None, :, None])
    own_choice = jnp.take(chosen_node.reshape(slot_count * DRAFT, DRAFT), row_pos, axis=0)
    spread = same_slot & jnp.tile(own_choice, (1, slot_count))
    accepted = jnp.dot(
        spread.astype(jnp.bfloat16), all_kv, preferred_element_type=jnp.float32
    ).astype(jnp.bfloat16)
    return (attn_own, layer_out, accepted)


def solution(mesh):
    in_specs = (
        P(("req", "tp"), None),
        P(("req", "tp"), None),
        P(("req", "tp"), None),
        P("req"),
        P("req"),
        P("req", None, "tp"),
        P(("req", "tp"), None, None),
        P(("req", "tp"), None, None),
        P("req", None),
        P("req"),
        P(),
        P(),
        P(),
        P("req", None),
        P("tp", None, None),
        P("tp", None, None),
    )
    out_specs = (P(("req", "tp"), None), P(("req", "tp"), None), P(("req", "tp"), None))
    return jax.shard_map(
        per_device, mesh=mesh, in_specs=in_specs, out_specs=out_specs, check_vma=False
    )
```

profile of v0, /device:TPU:8, one launch (start us, length us, event | category | flops | bytes accessed | tf_op | source)
XLA Modules:
  0.0 735.7 jit_solution(6289044526441213164)
XLA Ops:
  12.0 13.2 %all-gather = bf16[8,4,1536]{2,1,0:T(4,128)(2,1)S(1)} all-gather(bf16[1,4,1536]{2,1,0:T(4,128)(2,1)} %bitcast.182), channel_id=1, replica_groups=mesh['req'=8,'tp'=32] {'req'}, dimensions={0}, use_global_device_ids=true | all-gather | bytes 110592 | tf_op jit(solution)/shard_map/all_gather | solution.py:121
  30.7 52.7 %all-gather.1 = bf16[32,4,1536]{2,1,0:T(4,128)(2,1)S(1)} all-gather(bf16[1,4,1536]{2,1,0:T(4,128)(2,1)S(1)} %fusion.72), channel_id=1, replica_groups=mesh['req'=8,'tp'=32] {'tp'}, dimensions={0}, use_global_device_ids=true | all-gather | bytes 405504 | tf_op jit(solution)/shard_map/all_gather | solution.py:135
  85.0 2.0 bitcast_reduce_fusion
  88.3 1.8 copy.183
  90.1 2.4 convert_reduce_fusion
  105.8 13.0 %all-gather.2 = bf16[8,4,1024]{2,1,0:T(4,128)(2,1)S(1)} all-gather(bf16[1,4,1024]{2,1,0:T(4,128)(2,1)} %bitcast.184), channel_id=1, replica_groups=mesh['req'=8,'tp'=32] {'req'}, dimensions={0}, use_global_device_ids=true | all-gather | bytes 73728 | tf_op jit(solution)/shard_map/all_gather | solution.py:122
  119.5 48.1 %all-gather.3 = bf16[32,4,1024]{2,1,0:T(4,128)(2,1)S(1)} all-gather(bf16[1,4,1024]{2,1,0:T(4,128)(2,1)S(1)} %select_bitcast_fusion), channel_id=1, replica_groups=mesh['req'=8,'tp'=32] {'tp'}, dimensions={0}, use_global_device_ids=true | all-gather | bytes 270336 | tf_op jit(solution)/shard_map/all_gather | solution.py:136
  173.7 3.4 dynamic_update_slice.14
  178.9 12.7 %all-gather.4 = bf16[8,4,1536]{2,1,0:T(4,128)(2,1)S(1)} all-gather(bf16[1,4,1536]{2,1,0:T(4,128)(2,1)S(1)} %bitcast.183), channel_id=1, replica_groups=mesh['req'=8,'tp'=32] {'req'}, dimensions={0}, use_global_device_ids=true | all-gather | bytes 110592 | tf_op jit(solution)/shard_map/all_gather | solution.py:123
  193.7 52.7 %all_gather.46 = f32[32,128,24]{1,2,0:T(8,128)} all-gather(f32[1,128,24]{1,2,0:T(8,128)S(1)} %dynamic_update_slice.12), channel_id=1, replica_groups=mesh['req'=8,'tp'=32] {'tp'}, dimensions={0}, use_global_device_ids=true | all-gather | bytes 405504 | tf_op jit(solution)/shard_map/all_gather | solution.py:18
  246.4 53.1 %all_gather.48 = f32[32,128,24]{1,2,0:T(8,128)} all-gather(f32[1,128,24]{1,2,0:T(8,128)S(1)} %dynamic_update_slice.13), channel_id=1, replica_groups=mesh['req'=8,'tp'=32] {'tp'}, dimensions={0}, use_global_device_ids=true | all-gather | bytes 405504 | tf_op jit(solution)/shard_map/all_gather | solution.py:18
  302.2 61.5 %all-gather.8.cloned.1.call-done = f32[32,128,1536]{2,1,0:T(8,128)} async-done(((f32[1,128,1536]{2,1,0:T(8,128)}), f32[32,128,1536]{2,1,0:T(8,128)}) %all-gather.8.cloned.1.call-update) | async-done | bytes 25165840 | tf_op jit(solution)/shard_map/all_gather | solution.py:18
  366.1 156.1 %while.19 = (s32[]{:T(128)}, f32[128,24]{0,1:T(8,128)}, f32[128,24]{0,1:T(8,128)}, f32[128,1536]{0,1:T(8,128)}, f32[32,128,24]{1,2,0:T(8,128)}, /*index=5*/f32[3...) while((s32[]{:T(128)}, f32[128,24]{0,1:T(8,128)}, f32[128,24]{0,1:T(8,128)}, ...), condition=%wide.region_6.9_spmd, body=%wide.region_5.8_spmd.sunk | while | flops 608261 | bytes 5628047 | solution.py:23
  368.9 2.2 fusion.76
  373.9 2.2 fusion.76
  379.0 2.2 fusion.76
  384.0 2.2 fusion.76
  389.0 2.2 fusion.76
  394.1 2.2 fusion.76
  399.1 2.2 fusion.76
  404.2 2.2 fusion.76
  409.2 2.2 fusion.76
  414.2 2.2 fusion.76
  419.3 2.2 fusion.76
  424.3 2.2 fusion.76
  429.3 2.2 fusion.76
  434.4 2.2 fusion.76
  439.4 2.2 fusion.76
  444.4 2.2 fusion.76
  449.5 2.2 fusion.76
  454.5 2.2 fusion.76
  459.6 2.2 fusion.76
  464.6 2.2 fusion.76
  469.6 2.2 fusion.76
  474.7 2.2 fusion.76
  479.7 2.2 fusion.76
  484.7 2.2 fusion.76
  489.8 2.2 fusion.76
  494.8 2.2 fusion.76
  499.9 2.2 fusion.76
  504.9 2.2 fusion.76
  509.9 2.2 fusion.76
  515.0 2.2 fusion.76
  520.0 2.2 fusion.76
  524.7 3.2 multiply_reduce_fusion
  528.0 47.5 %all-gather.5 = bf16[32,4,1536]{2,1,0:T(4,128)(2,1)S(1)} all-gather(bf16[1,4,1536]{2,1,0:T(4,128)(2,1)S(1)} %fusion.30), channel_id=1, replica_groups=mesh['req'=8,'tp'=32] {'tp'}, dimensions={0}, use_global_device_ids=true | all-gather | bytes 405504 | tf_op jit(solution)/shard_map/all_gather | solution.py:215
  576.3 2.8 fusion.44
  582.8 144.7 %all-reduce.3.cloned.1.call-done = f32[128,1536]{1,0:T(8,128)} async-done(((f32[128,1536]{1,0:T(8,128)}), f32[128,1536]{1,0:T(8,128)}) %all-reduce.3.cloned.1.call-update) | async-done | bytes 786448
  (280 shorter events, 136.8 us)
Async XLA Ops:
  7.2 571.9 %copy-start = (bf16[5,128,1536]{2,1,0:T(8,128)(2,1)S(1)}, bf16[5,128,1536]{2,1,0:T(8,128)(2,1)}, u32[]{:S(2)}) copy-start(bf16[5,128,1536]{2,1,0:T(8,128)(2,1)} %param.37) | copy-start | bytes 5898244
  7.2 356.5 %all-gather.8.cloned.1.call-start = ((), (), s32[]{:S(2)}) async-start(), calls=%async_computation | async-start | bytes 25952256 | tf_op jit(solution)/shard_map/all_gather | solution.py:18
  7.2 3.6 copy-start.26
  11.4 107.9 %copy-start.20 = (pred[4]{0:T(512)(128)(4,1)}, pred[4]{0:T(512)(128)(4,1)S(1)}, u32[]{:S(2)}) copy-start(pred[4]{0:T(512)(128)(4,1)S(1)} %get-tuple-element.230) | copy-start | bytes 16
  12.0 13.9 %copy-start.22 = (s32[1024]{0:T(1024)}, s32[1024]{0:T(1024)S(1)}, u32[]{:S(2)}) copy-start(s32[1024]{0:T(1024)S(1)} %pad_clamp_fusion.2) | copy-start | bytes 12292
  29.0 55.9 %copy-start.31 = (s32[2]{0:T(128)S(1)}, s32[2]{0:T(128)}, u32[]{:S(2)}) copy-start(s32[2]{0:T(128)} %param.26) | copy-start | bytes 28
  85.0 3.2 copy-start.23
  87.0 0.6 copy-start.5
  90.1 2.4 copy-start.2
  90.1 2.4 copy-start.6
  90.1 2.4 copy-start.11
  90.1 2.4 copy-start.24
  102.0 66.0 %copy-start.27 = (s32[4]{0:T(128)S(1)}, s32[4]{0:T(128)}, u32[]{:S(2)}) copy-start(s32[4]{0:T(128)} %copy-done.26) | copy-start | bytes 52
  102.0 66.0 %copy-start.29 = (s32[128]{0:T(128)S(1)}, s32[128]{0:T(128)}, u32[]{:S(2)}) copy-start(s32[128]{0:T(128)} %and_select_fusion.1) | copy-start | bytes 1540
  103.9 65.1 %copy-start.7 = (f32[2,64,8,3]{1,0,3,2:T(2,128)S(1)}, f32[2,64,8,3]{1,0,3,2:T(2,128)}, u32[]{:S(2)}) copy-start(f32[2,64,8,3]{1,0,3,2:T(2,128)} %copy.169) | copy-start | bytes 36868
  118.7 50.5 %copy-start.12 = (f32[2,64,8,3]{1,3,2,0:T(4,128)S(1)}, f32[2,64,8,3]{1,3,2,0:T(4,128)}, u32[]{:S(2)}) copy-start(f32[2,64,8,3]{1,3,2,0:T(4,128)} %convert_reduce_fusion) | copy-start | bytes 36868
  167.7 2.5 copy-start.3
  169.2 0.9 copy-start.9
  170.9 2.9 copy-start.1
  177.2 1.5 copy-start.8
  177.2 1.6 copy-start.10
  177.2 1.7 copy-start.17
  177.2 15.7 %copy-start.19 = (f32[1,4,24]{2,1,0:T(4,128)S(1)}, f32[1,4,24]{2,1,0:T(4,128)}, u32[]{:S(2)}) copy-start(f32[1,4,24]{2,1,0:T(4,128)} %get-tuple-element.236) | copy-start | bytes 1156
  178.5 549.0 %all-reduce.3.cloned.1.call-start = ((), (), s32[]{:S(2)}) async-start(), calls=%async_computation.1 | async-start | bytes 1572864
  522.2 2.5 copy-start.14
  522.2 2.5 copy-start.21
  524.7 3.2 copy-start.15
  524.7 3.2 copy-start.18
  527.9 47.8 %copy-start.13 = (bf16[1536,40]{0,1:T(8,128)(2,1)S(1)}, bf16[1536,40]{0,1:T(8,128)(2,1)}, u32[]{:S(2)}) copy-start(bf16[1536,40]{0,1:T(8,128)(2,1)} %param.34) | copy-start | bytes 368644
  527.9 48.0 %copy-start.16 = (s32[128,8]{0,1:T(8,128)S(1)}, s32[128,8]{0,1:T(8,128)}, u32[]{:S(2)}) copy-start(s32[128,8]{0,1:T(8,128)} %param.35) | copy-start | bytes 12292
  579.1 1.5 copy-start.25
  579.1 1.6 copy-start.32
  579.1 2.8 copy-start.4
  579.1 2.8 copy-start.28
  579.1 2.8 copy-start.30
Sparse Core Ops, SparseCore 0:
  178.6 184.9 all-gather.7
  580.7 146.7 all-reduce.2
where the time goes:
time: 741 us; the launch traced here: 736 us
  blocking collectives  293 us (40%)
  waiting for transfers between devices  206 us (28%)
  other arithmetic  128 us (17%)
  local copies, waits for them, and re-layouts  78.3 us (11%)
  between operations  15.4 us (2%)
  matrix products  14.5 us (2%)
    unnamed x3, waiting for transfers between devices  145 us
    all_gather x2, blocking collectives, joined_2(): gathered = jax.tree.map(lambda a: lax.all_gather(a, axis), part)  106 us
    add x32, other arithmetic, combine_stats(): left_out.reshape(row_count, head_count, -1) * left_scale[..., None]  70.1 us
    all_gather x1, waiting for transfers between devices, joined_2(): gathered = jax.tree.map(lambda a: lax.all_gather(a, axis), part)  61.5 us
    all_gather x1, blocking collectives, per_device(): lax.all_gather(own_q, 'tp', axis=0, tiled=True)  52.7 us
    all_gather x1, blocking collectives, per_device(): lax.all_gather(own_kv, 'tp', axis=0, tiled=True)  48.1 us
    all_gather x1, blocking collectives, per_device(): normed_all = lax.all_gather(normed_own, 'tp', axis=0, tiled=True)  47.5 us
    dynamic_slice x62, local copies, waits for them, and re-layouts, take(): lax.dynamic_index_in_dim(a, source, 0, False)  44.7 us
  transfers between devices with their start and end apart: 2, of which 2 were waited for; matrix products, arithmetic and copies ran while one was open for 1% of the time, Pallas kernels for 0%

commit v1 on v0

--- a/solution.py
+++ b/solution.py
@@ -133,7 +133,9 @@
     own_res = jnp.take(pulled_res, source_rows, axis=0)
     all_q, all_kv = (
         lax.all_gather(own_q, "tp", axis=0, tiled=True),
-        lax.all_gather(own_kv, "tp", axis=0, tiled=True),
+        jnp.concatenate(
+            lax.all_to_all(jnp.stack([own_kv] * lax.axis_size("tp")), "tp", 0, 0), axis=0
+        ),
     )
     local_pages = page_table.shape[1]
     page_ids = page_table[:, :, 0].reshape(-1)

time: 741 us -> 702 us (0.947)
  blocking collectives: 293 us -> 243 us
  starting transfers between devices: 0.26 us -> 11.5 us
    all_gather x1 -> x0, blocking collectives: 48.1 us -> none  [per_device(): lax.all_gather(own_kv, 'tp', axis=0, tiled=True)]
    all_to_all x0 -> x1, starting transfers between devices: none -> 11.4 us  [per_device(): lax.all_to_all(jnp.stack([own_kv] * lax.axis_size('tp')), 'tp', 0, 0)]
  transfers between devices with their start and end apart: 2 -> 3, of which waited for: 2 -> 2; matrix products, arithmetic and copies ran while one was open for 1% -> 5% of each run, Pallas kernels for 0% -> 0%
where the time goes in v1:
time: 702 us; the launch traced here: 697 us
  blocking collectives  243 us (35%)
  waiting for transfers between devices  207 us (29%)
  other arithmetic  127 us (18%)
  local copies, waits for them, and re-layouts  79 us (11%)
  between operations  15.4 us (2%)
  matrix products  14.4 us (2%)
  starting transfers between devices  11.5 us (2%)
    unnamed x3, waiting for transfers between devices  145 us
    all_gather x2, blocking collectives, joined_2(): gathered = jax.tree.map(lambda a: lax.all_gather(a, axis), part)  106 us
    add x32, other arithmetic, combine_stats(): left_out.reshape(row_count, head_count, -1) * left_scale[..., None]  70.1 us
    all_gather x1, waiting for transfers between devices, joined_2(): gathered = jax.tree.map(lambda a: lax.all_gather(a, axis), part)  61.9 us
    all_gather x1, blocking collectives, per_device(): lax.all_gather(own_q, 'tp', axis=0, tiled=True)  50.1 us
    all_gather x1, blocking collectives, per_device(): normed_all = lax.all_gather(normed_own, 'tp', axis=0, tiled=True)  47.5 us
    dynamic_slice x62, local copies, waits for them, and re-layouts, take(): lax.dynamic_index_in_dim(a, source, 0, False)  44.7 us
    add x31, other arithmetic, combine_stats(): left_sum * left_scale + right_sum * right_scale  42.5 us
  transfers between devices with their start and end apart: 3, of which 2 were waited for; matrix products, arithmetic and copies ran while one was open for 5% of the time, Pallas kernels for 0%

profile of v1, /device:TPU:8, one launch (start us, length us, event | category | flops | bytes accessed | tf_op | source)
XLA Modules:
  0.0 696.9 jit_solution(16843362347382196441)
XLA Ops:
  8.2 13.2 %all-gather.2 = bf16[8,4,1024]{2,1,0:T(4,128)(2,1)S(1)} all-gather(bf16[1,4,1024]{2,1,0:T(4,128)(2,1)} %bitcast.183), channel_id=1, replica_groups=mesh['req'=8,'tp'=32] {'req'}, dimensions={0}, use_global_device_ids=true | all-gather | bytes 73728 | tf_op jit(solution)/shard_map/all_gather | solution.py:122
  22.9 11.4 %all-to-all-start = ((bf16[32,4,1024]{2,1,0:T(4,128)(2,1)}), bf16[32,4,1024]{2,1,0:T(4,128)(2,1)}, u32[]{:S(2)}, u32[]{:S(2)}) async-start(bf16[32,4,1024]{2,1,0:T(4,128)(2,1)} %stack.2), calls=%async_computation | async-start | bytes 524288 | tf_op jit(solution)/shard_map/all_to_all | solution.py:137
  37.2 12.9 %all-gather = bf16[8,4,1536]{2,1,0:T(4,128)(2,1)S(1)} all-gather(bf16[1,4,1536]{2,1,0:T(4,128)(2,1)} %bitcast.181), channel_id=1, replica_groups=mesh['req'=8,'tp'=32] {'req'}, dimensions={0}, use_global_device_ids=true | all-gather | bytes 110592 | tf_op jit(solution)/shard_map/all_gather | solution.py:121
  53.8 50.1 %all-gather.1 = bf16[32,4,1536]{2,1,0:T(4,128)(2,1)S(1)} all-gather(bf16[1,4,1536]{2,1,0:T(4,128)(2,1)S(1)} %fusion.71), channel_id=1, replica_groups=mesh['req'=8,'tp'=32] {'tp'}, dimensions={0}, use_global_device_ids=true | all-gather | bytes 405504 | tf_op jit(solution)/shard_map/all_gather | solution.py:135
  105.6 2.0 bitcast_reduce_fusion
  110.6 2.4 convert_reduce_fusion
  115.2 1.8 reshape.525
  133.7 3.4 dynamic_update_slice.14
  138.7 12.9 %all-gather.3 = bf16[8,4,1536]{2,1,0:T(4,128)(2,1)S(1)} all-gather(bf16[1,4,1536]{2,1,0:T(4,128)(2,1)S(1)} %bitcast.182), channel_id=1, replica_groups=mesh['req'=8,'tp'=32] {'req'}, dimensions={0}, use_global_device_ids=true | all-gather | bytes 110592 | tf_op jit(solution)/shard_map/all_gather | solution.py:123
  154.1 53.7 %all_gather.42 = f32[32,128,24]{1,2,0:T(8,128)} all-gather(f32[1,128,24]{1,2,0:T(8,128)S(1)} %dynamic_update_slice.12), channel_id=1, replica_groups=mesh['req'=8,'tp'=32] {'tp'}, dimensions={0}, use_global_device_ids=true | all-gather | bytes 405504 | tf_op jit(solution)/shard_map/all_gather | solution.py:18
  207.7 52.5 %all_gather.44 = f32[32,128,24]{1,2,0:T(8,128)} all-gather(f32[1,128,24]{1,2,0:T(8,128)S(1)} %dynamic_update_slice.13), channel_id=1, replica_groups=mesh['req'=8,'tp'=32] {'tp'}, dimensions={0}, use_global_device_ids=true | all-gather | bytes 405504 | tf_op jit(solution)/shard_map/all_gather | solution.py:18
  262.8 61.9 %all-gather.7.cloned.1.call-done = f32[32,128,1536]{2,1,0:T(8,128)} async-done(((f32[1,128,1536]{2,1,0:T(8,128)}), f32[32,128,1536]{2,1,0:T(8,128)}) %all-gather.7.cloned.1.call-update) | async-done | bytes 25165840 | tf_op jit(solution)/shard_map/all_gather | solution.py:18
  327.2 156.1 %while.19 = (s32[]{:T(128)}, f32[128,24]{0,1:T(8,128)}, f32[128,24]{0,1:T(8,128)}, f32[128,1536]{0,1:T(8,128)}, f32[32,128,24]{1,2,0:T(8,128)}, /*index=5*/f32[3...) while((s32[]{:T(128)}, f32[128,24]{0,1:T(8,128)}, f32[128,24]{0,1:T(8,128)}, ...), condition=%wide.region_6.9_spmd, body=%wide.region_5.8_spmd.sunk | while | flops 608261 | bytes 5628047 | solution.py:23
  330.0 2.2 fusion.75
  335.0 2.2 fusion.75
  340.1 2.2 fusion.75
  345.1 2.2 fusion.75
  350.2 2.2 fusion.75
  355.2 2.2 fusion.75
  360.2 2.2 fusion.75
  365.3 2.2 fusion.75
  370.3 2.2 fusion.75
  375.3 2.2 fusion.75
  380.4 2.2 fusion.75
  385.4 2.2 fusion.75
  390.4 2.2 fusion.75
  395.5 2.2 fusion.75
  400.5 2.2 fusion.75
  405.6 2.2 fusion.75
  410.6 2.2 fusion.75
  415.6 2.2 fusion.75
  420.7 2.2 fusion.75
  425.7 2.2 fusion.75
  430.7 2.2 fusion.75
  435.8 2.2 fusion.75
  440.8 2.2 fusion.75
  445.9 2.2 fusion.75
  450.9 2.2 fusion.75
  455.9 2.2 fusion.75
  461.0 2.2 fusion.75
  466.0 2.2 fusion.75
  471.0 2.2 fusion.75
  476.1 2.2 fusion.75
  481.1 2.2 fusion.75
  485.8 3.2 multiply_reduce_fusion
  489.2 47.5 %all-gather.4 = bf16[32,4,1536]{2,1,0:T(4,128)(2,1)S(1)} all-gather(bf16[1,4,1536]{2,1,0:T(4,128)(2,1)S(1)} %fusion.30), channel_id=1, replica_groups=mesh['req'=8,'tp'=32] {'tp'}, dimensions={0}, use_global_device_ids=true | all-gather | bytes 405504 | tf_op jit(solution)/shard_map/all_gather | solution.py:217
  537.4 2.8 fusion.42
  544.0 144.7 %all-reduce.3.cloned.1.call-done = f32[128,1536]{1,0:T(8,128)} async-done(((f32[128,1536]{1,0:T(8,128)}), f32[128,1536]{1,0:T(8,128)}) %all-reduce.3.cloned.1.call-update) | async-done | bytes 786448
  (279 shorter events, 136.3 us)
Async XLA Ops:
  7.2 533.1 %copy-start = (bf16[5,128,1536]{2,1,0:T(8,128)(2,1)S(1)}, bf16[5,128,1536]{2,1,0:T(8,128)(2,1)}, u32[]{:S(2)}) copy-start(bf16[5,128,1536]{2,1,0:T(8,128)(2,1)} %param.37) | copy-start | bytes 5898244
  7.2 43.8 %copy-start.7 = (bf16[2,128,512]{2,1,0:T(8,128)(2,1)S(1)}, bf16[2,128,512]{2,1,0:T(8,128)(2,1)}, u32[]{:S(2)}) copy-start(bf16[2,128,512]{2,1,0:T(8,128)(2,1)} %param.29) | copy-start | bytes 786436
  7.2 44.4 %copy-start.8 = (bf16[2,128,512]{2,1,0:T(8,128)(2,1)S(1)}, bf16[2,128,512]{2,1,0:T(8,128)(2,1)}, u32[]{:S(2)}) copy-start(bf16[2,128,512]{2,1,0:T(8,128)(2,1)} %param.28) | copy-start | bytes 786436
  7.2 43.7 %copy-start.24 = (s32[4]{0:T(128)}, s32[4]{0:T(128)S(1)}, u32[]{:S(2)}) copy-start(s32[4]{0:T(128)S(1)} %and_select_fusion.4) | copy-start | bytes 52
  8.2 42.8 %copy-start.21 = (pred[4]{0:T(512)(128)(4,1)}, pred[4]{0:T(512)(128)(4,1)S(1)}, u32[]{:S(2)}) copy-start(pred[4]{0:T(512)(128)(4,1)S(1)} %get-tuple-element.230) | copy-start | bytes 16
  22.9 104.4 %all-to-all-start = ((bf16[32,4,1024]{2,1,0:T(4,128)(2,1)}), bf16[32,4,1024]{2,1,0:T(4,128)(2,1)}, u32[]{:S(2)}, u32[]{:S(2)}) async-start(bf16[32,4,1024]{2,1,0:T(4,128)(2,1)} %stack.2), calls=%async_computation | async-start | bytes 524288 | tf_op jit(solution)/shard_map/all_to_all | solution.py:137
  34.3 290.4 %all-gather.7.cloned.1.call-start = ((), (), s32[]{:S(2)}) async-start(), calls=%async_computation.1 | async-start | bytes 25952256 | tf_op jit(solution)/shard_map/all_gather | solution.py:18
  37.2 13.7 %copy-start.23 = (s32[1024]{0:T(1024)}, s32[1024]{0:T(1024)S(1)}, u32[]{:S(2)}) copy-start(s32[1024]{0:T(1024)S(1)} %pad_clamp_fusion.2) | copy-start | bytes 12292
  52.2 53.3 %copy-start.28 = (s32[2]{0:T(128)S(1)}, s32[2]{0:T(128)}, u32[]{:S(2)}) copy-start(s32[2]{0:T(128)} %param.26) | copy-start | bytes 28
  107.5 0.6 copy-start.5
  110.6 2.4 copy-start.4
  110.6 2.4 copy-start.6
  110.6 2.4 copy-start.12
  117.0 9.9 %copy-start.25 = (s32[4]{0:T(128)S(1)}, s32[4]{0:T(128)}, u32[]{:S(2)}) copy-start(s32[4]{0:T(128)} %copy-done.24) | copy-start | bytes 52
  118.8 7.8 %copy-start.13 = (f32[2,64,8,3]{1,3,2,0:T(4,128)S(1)}, f32[2,64,8,3]{1,3,2,0:T(4,128)}, u32[]{:S(2)}) copy-start(f32[2,64,8,3]{1,3,2,0:T(4,128)} %convert_reduce_fusion) | copy-start | bytes 36868
  126.7 0.6 copy-start.10
  128.3 1.9 copy-start.2
  130.9 2.9 copy-start.1
  137.1 1.4 copy-start.9
  137.2 1.5 copy-start.11
  137.2 1.5 copy-start.18
  137.2 16.3 %copy-start.20 = (f32[1,4,24]{2,1,0:T(4,128)S(1)}, f32[1,4,24]{2,1,0:T(4,128)}, u32[]{:S(2)}) copy-start(f32[1,4,24]{2,1,0:T(4,128)} %get-tuple-element.236) | copy-start | bytes 1156
  138.5 550.2 %all-reduce.3.cloned.1.call-start = ((), (), s32[]{:S(2)}) async-start(), calls=%async_computation.2 | async-start | bytes 1572864
  483.3 2.5 copy-start.15
  483.3 2.5 copy-start.22
  485.8 3.2 copy-start.16
  485.8 3.2 copy-start.19
  489.0 47.9 %copy-start.14 = (bf16[1536,40]{0,1:T(8,128)(2,1)S(1)}, bf16[1536,40]{0,1:T(8,128)(2,1)}, u32[]{:S(2)}) copy-start(bf16[1536,40]{0,1:T(8,128)(2,1)} %param.34) | copy-start | bytes 368644
  489.0 48.1 %copy-start.17 = (s32[128,8]{0,1:T(8,128)S(1)}, s32[128,8]{0,1:T(8,128)}, u32[]{:S(2)}) copy-start(s32[128,8]{0,1:T(8,128)} %param.35) | copy-start | bytes 12292
  489.1 48.2 %copy-start.30 = (s32[5]{0:T(128)S(1)}, s32[5]{0:T(128)}, u32[]{:S(2)}) copy-start(s32[5]{0:T(128)} %and_select_fusion.1) | copy-start | bytes 64
  540.3 1.5 copy-start.26
  540.3 1.5 copy-start.27
  540.3 1.7 copy-start.29
  540.3 2.9 copy-start.3
Sparse Core Ops, SparseCore 0:
  138.6 186.1 all-gather.6
  541.9 146.6 all-reduce.2
